TPU v7x, 128 devices: a whole 4x4x4 slice. The times are simulated.
128 devices in a mesh: blk: 32 (over x, z, core), tok: 4 (over y).
Axes of the slice: x: 4, y: 4, z: 4, core: 2. Of those that a mesh axis runs over, the one named last changes fastest.
Arguments:
- stream: bfloat16 [16384, 1664], P(('tok', 'blk'))
- queries: bfloat16 [16384, 1664], P(('tok', 'blk'))
- key_cache: bfloat16 [16384, 1664], P(('tok', 'blk'))
- value_cache: bfloat16 [16384, 1664], P(('tok', 'blk')), may hold values from -6 to 6
- segments: int32 [16384], P('tok'), may hold values from 63 to 16383, as said below
- stale_rows: int32 [1536], P(('tok', 'blk')), may hold values from 0 to 16383, as said below
- owners: int32 [4096], P(('tok', 'blk')), may hold values from 0 to 3, as said below
- attn_gain: float32 [1664], replicated, may hold values from 0.1 to 1.9
- w_key: bfloat16 [1664, 1664], replicated, may hold values from -0.15625 to 0.15625
- key_bias: float32 [1664], replicated, may hold values from -3 to 3
- mlp_gain: float32 [1664], replicated, may hold values from 0.1 to 1.9
- w_fc: bfloat16 [1664, 8192], P(None, 'blk'), may hold values from -0.15625 to 0.15625
- b_fc: float32 [8192], P('blk'), may hold values from -3 to 3
- w_proj: bfloat16 [8192, 1664], P('blk'), may hold values from -0.125 to 0.125
- b_proj: float32 [1664], replicated, may hold values from -3 to 3
- merge_gain: float32 [1664], replicated, may hold values from 0.1 to 1.9
- w_merge: bfloat16 [1664, 1664], replicated, may hold values from -0.15625 to 0.15625
- b_merge: float32 [1664], replicated, may hold values from -3 to 3
Outputs:
- refreshed_keys: bfloat16 [16384, 1664], P(('tok', 'blk'))
- delivered: bfloat16 [4, 32, 128, 1664], P('tok', 'blk')
Inputs may be any that keep to these rules, and one draw needn't show every extreme that they name: `segments`: A segment's id is the index of its last row, so ids never fall; each segment has 4 to 128 rows, a multiple of 4, and lies inside one aligned block of 4096 rows; each such block begins with a segment of 64 rows followed by one of exactly 128 rows. `stale_rows`: Distinct; the aligned block of 128 rows of each device holds exactly 12 of them, all inside that block and listed on that device; row 0 and the last row are always listed. `owners`: all merged tokens of one segment (the segment of row 4 m for merged token m) have the same owner.
All inputs are finite; a program needn't handle non-finite values.
Results may differ from a plain program's by a relative error of at most 0.011.
Values may be sent and summed in bfloat16 or wider, within the bound.
No kernel may reach another device: no remote copies, remote signals or barrier semaphores. Data moves between devices by JAX's collectives and lax.ppermute only.
A program may use at most 192 MiB of HBM per device.

v0:
```python
import jax
import jax.numpy as jnp
from jax import lax
from jax.sharding import PartitionSpec as P

HEADS = 16


def passed_along(block, axis, distance):
    devices = range(lax.axis_size(axis))
    route = [(i - distance, i) for i in devices if i - distance in devices]
    return lax.ppermute(block, axis, route)


def layer_norm(values, gain):
    center = values - jnp.mean(values, axis=-1, keepdims=True)
    spread = jnp.mean(center * center, axis=-1, keepdims=True)
    return center * lax.rsqrt(spread + 1e-06) * gain


def body(
    stream,
    queries,
    key_cache,
    value_cache,
    segments,
    stale_rows,
    owners,
    attn_gain,
    w_key,
    key_bias,
    mlp_gain,
    w_fc,
    b_fc,
    w_proj,
    b_proj,
    merge_gain,
    w_merge,
    b_merge,
):
    row_count = stream.shape[0]
    model_width = stream.shape[1]
    head_size = model_width // HEADS
    local_rows = stale_rows % row_count
    held = layer_norm(stream[local_rows].astype(jnp.float32), attn_gain).astype(jnp.bfloat16)
    fresh_keys = (jnp.dot(held, w_key, preferred_element_type=jnp.float32) + key_bias).astype(
        jnp.bfloat16
    )
    refreshed = key_cache.at[local_rows].set(fresh_keys)
    below = passed_along((refreshed, value_cache), "blk", 1)
    above = passed_along((refreshed, value_cache), "blk", -1)
    key_window = jnp.concatenate([below[0], refreshed, above[0]], axis=0).reshape(
        3 * row_count, HEADS, head_size
    )
    value_window = jnp.concatenate([below[1], value_cache, above[1]], axis=0).reshape(
        3 * row_count, HEADS, head_size
    )
    position = lax.axis_index("blk")
    minus_ones = jnp.full((row_count,), -1, jnp.int32)
    seg_padded = jnp.concatenate([minus_ones, segments, minus_ones], axis=0)
    key_seg = lax.dynamic_slice_in_dim(seg_padded, position * row_count, 3 * row_count, 0)
    query_seg = lax.dynamic_slice_in_dim(segments, position * row_count, row_count, 0)
    query_heads = queries.reshape(row_count, HEADS, head_size)
    scores = jnp.einsum(
        "qhd,khd->hqk", query_heads, key_window, preferred_element_type=jnp.float32
    ) * (1.0 / head_size**0.5)
    allowed = (query_seg[:, None] == key_seg[None, :])[None]
    scores = jnp.where(allowed, scores, -jnp.inf)
    top_score = jnp.max(scores, axis=-1, keepdims=True)
    weights = jnp.exp(scores - top_score)
    probs = (weights / jnp.sum(weights, axis=-1, keepdims=True)).astype(jnp.bfloat16)
    attended = jnp.einsum("hqk,khd->qhd", probs, value_window, preferred_element_type=jnp.float32)
    attended = attended.reshape(row_count, model_width).astype(jnp.bfloat16)
    mixed = stream.astype(jnp.float32) + attended.astype(jnp.float32)
    normed = layer_norm(mixed, mlp_gain).astype(jnp.bfloat16)
    group_units = jax.nn.gelu(
        jnp.dot(
            lax.all_gather(normed, "blk", axis=0, tiled=True),
            w_fc,
            preferred_element_type=jnp.float32,
        )
        + b_fc,
        approximate=False,
    ).astype(jnp.bfloat16)
    summed = lax.psum_scatter(
        jnp.dot(group_units, w_proj, preferred_element_type=jnp.float32).astype(jnp.bfloat16),
        "blk",
        scatter_dimension=0,
        tiled=True,
    ).astype(jnp.float32)
    pooled = jnp.mean((mixed + summed).reshape(row_count // 4, 4, model_width), axis=1) + b_proj
    merge_in = layer_norm(pooled, merge_gain).astype(jnp.bfloat16)
    merged = (jnp.dot(merge_in, w_merge, preferred_element_type=jnp.float32) + b_merge).astype(
        jnp.bfloat16
    )
    owner_count = lax.axis_size("tok")
    merged_rows = row_count // 4
    owner_hot = (owners[:, None] == jnp.arange(owner_count, dtype=jnp.int32)[None, :]).astype(
        jnp.int32
    )
    ranking = jnp.sum(jnp.cumsum(owner_hot, axis=0) * owner_hot, axis=-1) - 1
    selector = (
        owners[None, None, :] == jnp.arange(owner_count, dtype=jnp.int32)[:, None, None]
    ) & (ranking[None, None, :] == jnp.arange(merged_rows, dtype=jnp.int32)[None, :, None])
    outgoing = jnp.einsum(
        "osm,md->osd", selector.astype(jnp.bfloat16), merged, preferred_element_type=jnp.float32
    ).astype(jnp.bfloat16)
    arrived = lax.all_to_all(outgoing, "tok", split_axis=0, concat_axis=0, tiled=True)
    delivered = arrived.reshape(1, 1, owner_count * merged_rows, model_width)
    return (refreshed, delivered)


def solution(mesh):
    return jax.shard_map(
        body,
        mesh=mesh,
        in_specs=(
            P(("tok", "blk"), None),
            P(("tok", "blk"), None),
            P(("tok", "blk"), None),
            P(("tok", "blk"), None),
            P("tok"),
            P(("tok", "blk")),
            P(("tok", "blk")),
            P(),
            P(),
            P(),
            P(),
            P(None, "blk"),
            P("blk"),
            P("blk", None),
            P(),
            P(),
            P(),
            P(),
        ),
        out_specs=(P(("tok", "blk"), None), P("tok", "blk", None, None)),
        check_vma=False,
    )
```

profile of v0, /device:TPU:0, one launch (start us, length us, event | category | flops | bytes accessed | tf_op | source)
XLA Modules:
  0.0 274.7 jit_solution(774383592987161788)
XLA Ops:
  7.3 0.8 compare_select_fusion
  8.1 1.7 gather_fusion
  10.1 3.4 %fusion.14 = bf16[12,1664]{1,0:T(8,128)(2,1)S(1)} fusion(bf16[1664,1664]{1,0:T(8,128)(2,1)} %param.26, bf16[12,1664]{1,0:T(8,128)(2,1)S(1)} %gather_fusion, f32[1664]{0:T(1024)} %param.27, f32[1664]{0:T(1024)} %param.25, f32[12]{0:T(128)S(1)} %add_rsqrt_fusion.2, f32[12]{0:T(128)S(1)} %broadcast_multiply_fusion.2), kind=kOutput, calls=%fused_computation.33 | convolution fusion | flops 66593280 | bytes 5631072 | tf_op jit(solution)/shard_map/dot_general | solution.py:46
  13.6 0.9 scatter_fusion
  14.5 1.3 collective-permute-start.2
  15.9 1.3 collective-permute-start.3
  17.2 5.3 %collective-permute-start = (bf16[128,1664]{1,0:T(8,128)(2,1)S(1)}, bf16[128,1664]{1,0:T(8,128)(2,1)S(1)}, u32[]{:S(2)}, u32[]{:S(2)}) collective-permute-start(bf16[128,1664]{1,0:T(8,128)(2,1)S(1)} %copy-done.5), channel_id=1, source_target_pairs={{0,4},{4,8},{8,12},{12,16},{16,20},{20,24},{24,28},{28,32},{32,36}... | collective-permute-start | bytes 1277960 | tf_op jit(solution)/shard_map/ppermute | solution.py:12
  22.4 1.3 collective-permute-start.1
  23.8 1.0 copy.32
  25.1 0.7 copy-done.6
  25.8 1.2 pad_maximum_fusion.1
  27.0 1.5 copy.31
  28.6 1.1 pad_maximum_fusion
  29.7 1.6 copy.30
  31.3 4.4 %fusion.118 = (f32[16,128]{1,0:T(8,128)S(1)}, f32[16,128,384]{1,2,0:T(8,128)}) fusion(pred[128,384]{0,1:T(8,128)(4,1)S(1)} %broadcast_compare_fusion, bf16[384,16,104]{0,2,1:T(8,128)(2,1)} %bitcast.33, bf16[128,16,104]{0,2,1:T(8,128)(2,1)} %bitcast.36), kind=kOutput, calls=%fused_computation.159 | convolution fusion | flops 166723968 | bytes 4907008 | tf_op jit(solution)/shard_map/sub | solution.py:70
  35.7 2.5 fusion.52
  39.0 1.0 multiply_convert_fusion
  40.2 74.5 %all-gather.2.cloned.1.call-done = bf16[4096,1664]{1,0:T(8,128)(2,1)} async-done(((bf16[128,1664]{1,0:T(8,128)(2,1)}), bf16[4096,1664]{1,0:T(8,128)(2,1)}) %all-gather.2.cloned.1.call-update) | async-done | bytes 13631504 | tf_op jit(solution)/shard_map/all_gather | solution.py:78
  114.7 27.8 %convolution_convert_fusion = bf16[4096,1664]{1,0:T(8,128)(2,1)} fusion(bf16[256,1664]{1,0:T(8,128)(2,1)S(1)} %copy-done, bf16[4096,1664]{1,0:T(8,128)(2,1)} %all-gather.2.cloned.1.call-done, bf16[1664,256]{1,0:T(8,128)(2,1)S(1)} %copy-done.14, f32[256]{0:T(256)S(1)} %copy-done.15), kind=kOutput, calls=%fused_computation.3 | convolution fusion | flops 7055343616 | bytes 28967936 | tf_op jit(solution)/shard_map/dot_general | solution.py:86
  143.6 105.9 %reduce-scatter.2.cloned.1.call-done = bf16[128,1664]{1,0:T(8,128)(2,1)} async-done(((bf16[4096,1664]{1,0:T(8,128)(2,1)}), bf16[128,1664]{1,0:T(8,128)(2,1)}) %reduce-scatter.2.cloned.1.call-update) | async-done | bytes 426000 | tf_op jit(solution)/shard_map/reduce_scatter | solution.py:85
  249.4 1.1 convert_add_fusion
  251.7 3.8 %convolution_convert_fusion.1 = bf16[4,32,1664]{2,1,0:T(8,128)(2,1)S(1)} fusion(bf16[1664,1664]{1,0:T(8,128)(2,1)} %param.34, f32[32,1664]{1,0:T(8,128)S(1)} %reduce_sum.87, f32[1664]{0:T(1024)S(1)} %copy-done.11, f32[1664]{0:T(1024)S(1)} %copy-done.12, f32[32]{0:T(128)S(1)} %add_rsqrt_fusion, f32[32]{0:T(128)S(1)} %broadcast_multiply_fusion, ...), kind=kOutput, calls=%fused_computation.27 | convolution fusion | flops 191483904 | bytes 6198144 | tf_op jit(solution)/shard_map/osm,md->osd/dot_general | solution.py:105
  255.5 11.6 %all_to_all.5 = bf16[4,32,1664]{2,1,0:T(8,128)(2,1)S(1)} all-to-all(bf16[4,32,1664]{2,1,0:T(8,128)(2,1)S(1)} %convolution_convert_fusion.1), channel_id=1, replica_groups=mesh['blk'=32,'tok'=4] {'tok'}, dimensions={0} | all-to-all | bytes 851968 | tf_op jit(solution)/shard_map/all_to_all | solution.py:108
  267.1 0.8 copy.40
  (65 shorter events, 3.8 us)
Async XLA Ops:
  7.2 107.6 %copy-start = (bf16[256,1664]{1,0:T(8,128)(2,1)S(1)}, bf16[256,1664]{1,0:T(8,128)(2,1)}, u32[]{:S(2)}) copy-start(bf16[256,1664]{1,0:T(8,128)(2,1)} %param.31) | copy-start | bytes 2555908
  7.2 16.6 %copy-start.7 = (bf16[128,1664]{1,0:T(8,128)(2,1)S(1)}, bf16[128,1664]{1,0:T(8,128)(2,1)}, u32[]{:S(2)}) copy-start(bf16[128,1664]{1,0:T(8,128)(2,1)} %param.19) | copy-start | bytes 1277956
  7.2 6.4 %copy-start.3 = (bf16[128,1664]{1,0:T(8,128)(2,1)S(1)}, bf16[128,1664]{1,0:T(8,128)(2,1)}, u32[]{:S(2)}) copy-start(bf16[128,1664]{1,0:T(8,128)(2,1)} %param.20) | copy-start | bytes 1277956
  7.2 10.0 %copy-start.5 = (bf16[128,1664]{1,0:T(8,128)(2,1)S(1)}, bf16[128,1664]{1,0:T(8,128)(2,1)}, u32[]{:S(2)}) copy-start(bf16[128,1664]{1,0:T(8,128)(2,1)} %param.21) | copy-start | bytes 1277956
  7.2 107.5 %all-gather.2.cloned.1.call-start = ((), (), s32[]{:S(2)}) async-start(), calls=%async_computation.2 | async-start | bytes 14057472 | tf_op jit(solution)/shard_map/all_gather | solution.py:78
  7.3 17.5 %copy-start.9 = (s32[4096]{0:T(1024)S(1)}, s32[4096]{0:T(1024)}, u32[]{:S(2)}) copy-start(s32[4096]{0:T(1024)} %param.22) | copy-start | bytes 49156
  14.5 15.2 %copy-start.2 = (bf16[128,1664]{1,0:T(8,128)(2,1)}, bf16[128,1664]{1,0:T(8,128)(2,1)S(1)}, u32[]{:S(2)}) copy-start(bf16[128,1664]{1,0:T(8,128)(2,1)S(1)} %scatter_fusion) | copy-start | bytes 1277956
  14.5 10.5 %collective-permute-start.2 = (bf16[128,1664]{1,0:T(8,128)(2,1)S(1)}, bf16[128,1664]{1,0:T(8,128)(2,1)S(1)}, u32[]{:S(2)}, u32[]{:S(2)}) collective-permute-start(bf16[128,1664]{1,0:T(8,128)(2,1)S(1)} %scatter_fusion), channel_id=1, source_target_pairs={{0,4},{4,8},{8,12},{12,16},{16,20},{20,24},{24,28},{28,32},{32,36}... | collective-permute-start | bytes 1277960 | tf_op jit(solution)/shard_map/ppermute | solution.py:12
  15.9 9.9 %collective-permute-start.3 = (bf16[128,1664]{1,0:T(8,128)(2,1)S(1)}, bf16[128,1664]{1,0:T(8,128)(2,1)}, u32[]{:S(2)}, u32[]{:S(2)}) collective-permute-start(bf16[128,1664]{1,0:T(8,128)(2,1)S(1)} %scatter_fusion), channel_id=1, source_target_pairs={{4,0},{8,4},{12,8},{16,12},{20,16},{24,20},{28,24},{32,28},{36,32}... | collective-permute-start | bytes 1277960 | tf_op jit(solution)/shard_map/ppermute | solution.py:12
  17.2 11.4 %collective-permute-start = (bf16[128,1664]{1,0:T(8,128)(2,1)S(1)}, bf16[128,1664]{1,0:T(8,128)(2,1)S(1)}, u32[]{:S(2)}, u32[]{:S(2)}) collective-permute-start(bf16[128,1664]{1,0:T(8,128)(2,1)S(1)} %copy-done.5), channel_id=1, source_target_pairs={{0,4},{4,8},{8,12},{12,16},{16,20},{20,24},{24,28},{28,32},{32,36}... | collective-permute-start | bytes 1277960 | tf_op jit(solution)/shard_map/ppermute | solution.py:12
  22.4 6.1 %collective-permute-start.1 = (bf16[128,1664]{1,0:T(8,128)(2,1)S(1)}, bf16[128,1664]{1,0:T(8,128)(2,1)}, u32[]{:S(2)}, u32[]{:S(2)}) collective-permute-start(bf16[128,1664]{1,0:T(8,128)(2,1)S(1)} %copy-done.5), channel_id=1, source_target_pairs={{4,0},{8,4},{12,8},{16,12},{20,16},{24,20},{28,24},{32,28},{36,32}... | collective-permute-start | bytes 1277960 | tf_op jit(solution)/shard_map/ppermute | solution.py:12
  25.0 0.8 copy-start.6
  31.3 4.4 %copy-start.4 = (bf16[384,1664]{0,1:T(8,128)(2,1)S(1)}, bf16[384,1664]{0,1:T(8,128)(2,1)}, u32[]{:S(2)}) copy-start(bf16[384,1664]{0,1:T(8,128)(2,1)} %copy.30) | copy-start | bytes 3833860
  35.7 2.9 %copy-start.1 = (bf16[128,1664]{1,0:T(8,128)(2,1)S(1)}, bf16[128,1664]{1,0:T(8,128)(2,1)}, u32[]{:S(2)}) copy-start(bf16[128,1664]{1,0:T(8,128)(2,1)} %param.18) | copy-start | bytes 1277956
  38.2 0.8 copy-start.10
  38.2 76.5 %copy-start.15 = (f32[256]{0:T(256)S(1)}, f32[256]{0:T(256)}, u32[]{:S(2)}) copy-start(f32[256]{0:T(256)} %param.30) | copy-start | bytes 3076
  38.5 76.2 %copy-start.14 = (bf16[1664,256]{1,0:T(8,128)(2,1)S(1)}, bf16[1664,256]{1,0:T(8,128)(2,1)}, u32[]{:S(2)}) copy-start(bf16[1664,256]{1,0:T(8,128)(2,1)} %param.29) | copy-start | bytes 2555908
  40.0 209.4 %reduce-scatter.2.cloned.1.call-start = ((), (), s32[]{:S(2)}) async-start(), calls=%async_computation.3 | async-start | bytes 14057472 | tf_op jit(solution)/shard_map/reduce_scatter | solution.py:85
  142.6 0.7 copy-start.13
  143.2 108.1 %copy-start.8 = (f32[1664]{0:T(1024)S(1)}, f32[1664]{0:T(1024)}, u32[]{:S(2)}) copy-start(f32[1664]{0:T(1024)} %param.32) | copy-start | bytes 19972
  143.2 108.5 %copy-start.11 = (f32[1664]{0:T(1024)S(1)}, f32[1664]{0:T(1024)}, u32[]{:S(2)}) copy-start(f32[1664]{0:T(1024)} %param.35) | copy-start | bytes 19972
  143.2 108.5 %copy-start.12 = (f32[1664]{0:T(1024)S(1)}, f32[1664]{0:T(1024)}, u32[]{:S(2)}) copy-start(f32[1664]{0:T(1024)} %param.33) | copy-start | bytes 19972
Sparse Core Ops, SparseCore 0:
  40.1 74.5 all-gather.1
  142.7 106.6 reduce-scatter.1
where the time goes:
time: 275 us
  waiting for transfers between devices  180 us (65%)
  matrix products  42 us (15%)
  between operations  14.3 us (5%)
  blocking collectives  11.6 us (4%)
  local copies, waits for them, and re-layouts  9.54 us (3%)
  starting transfers between devices  9.43 us (3%)
  other arithmetic  7.38 us (3%)
    reduce_scatter x1, waiting for transfers between devices, body(): lax.psum_scatter(jnp.dot(group_units, w_proj, preferred_element_type=jnp....  106 us
    all_gather x1, waiting for transfers between devices, body(): lax.all_gather(normed, 'blk', axis=0, tiled=True)  74.5 us
    dot_general x1, matrix products, body(): jnp.dot(group_units, w_proj, preferred_element_type=jnp.float32)  27.8 us
    all_to_all x1, blocking collectives, body(): lax.all_to_all(outgoing, 'tok', split_axis=0, concat_axis=0, tiled=True)  11.6 us
    ppermute x4, starting transfers between devices, passed_along(): return lax.ppermute(block, axis, route)  9.17 us
  transfers between devices with their start and end apart: 6, of which 2 were waited for; matrix products, arithmetic and copies ran while one was open for 2% of the time, Pallas kernels for 0%

commit v1 on v0

--- a/solution.py
+++ b/solution.py
@@ -4,6 +4,12 @@
 from jax.sharding import PartitionSpec as P
 
 HEADS = 16
+
+
+def tiled_gather(x, axis, dim):
+    devices = lax.axis_size(axis)
+    repeats = [devices if d == dim else 1 for d in range(x.ndim)]
+    return lax.all_to_all(jnp.tile(x, repeats), axis, split_axis=dim, concat_axis=dim, tiled=True)
 
 
 def passed_along(block, axis, distance):
@@ -74,12 +80,7 @@
     mixed = stream.astype(jnp.float32) + attended.astype(jnp.float32)
     normed = layer_norm(mixed, mlp_gain).astype(jnp.bfloat16)
     group_units = jax.nn.gelu(
-        jnp.dot(
-            lax.all_gather(normed, "blk", axis=0, tiled=True),
-            w_fc,
-            preferred_element_type=jnp.float32,
-        )
-        + b_fc,
+        jnp.dot(tiled_gather(normed, "blk", 0), w_fc, preferred_element_type=jnp.float32) + b_fc,
         approximate=False,
     ).astype(jnp.bfloat16)
     summed = lax.psum_scatter(

time: 275 us -> 372 us (1.35)
  blocking collectives: 11.6 us -> 179 us
  waiting for transfers between devices: 180 us -> 105 us
  local copies, waits for them, and re-layouts: 9.54 us -> 16.1 us
    all_to_all x0 -> x1, blocking collectives: none -> 167 us  [tiled_gather(): lax.all_to_all(jnp.tile(x, repeats), axis, split_axis=dim, concat_axis=di...]
    all_gather x1 -> x0, waiting for transfers between devices: 74.5 us -> none  [body(): lax.all_gather(normed, 'blk', axis=0, tiled=True)]
    another operation x0 -> x1, local copies, waits for them, and re-layouts: none -> 6.59 us  [tiled_gather(): jnp.tile(x, repeats)]
  transfers between devices with their start and end apart: 6 -> 5, of which waited for: 2 -> 1; matrix products, arithmetic and copies ran while one was open for 2% -> 1% of each run, Pallas kernels for 0% -> 0%
where the time goes in v1:
time: 372 us
  blocking collectives  179 us (48%)
  waiting for transfers between devices  105 us (28%)
  matrix products  42 us (11%)
  local copies, waits for them, and re-layouts  16.1 us (4%)
  between operations  14.3 us (4%)
  starting transfers between devices  9.21 us (2%)
  other arithmetic  6.62 us (2%)
    all_to_all x1, blocking collectives, tiled_gather(): lax.all_to_all(jnp.tile(x, repeats), axis, split_axis=dim, concat_axis=di...  167 us
    reduce_scatter x1, waiting for transfers between devices, body(): lax.psum_scatter(jnp.dot(group_units, w_proj, preferred_element_type=jnp....  105 us
    dot_general x1, matrix products, body(): jnp.dot(group_units, w_proj, preferred_element_type=jnp.float32)  27.8 us
    all_to_all x1, blocking collectives, body(): lax.all_to_all(outgoing, 'tok', split_axis=0, concat_axis=0, tiled=True)  11.6 us
    ppermute x4, starting transfers between devices, passed_along(): return lax.ppermute(block, axis, route)  9.17 us
  transfers between devices with their start and end apart: 5, of which 1 were waited for; matrix products, arithmetic and copies ran while one was open for 1% of the time, Pallas kernels for 0%

profile of v1, /device:TPU:0, one launch (start us, length us, event | category | flops | bytes accessed | tf_op | source)
XLA Modules:
  0.0 371.5 jit_solution(14682407387627105649)
XLA Ops:
  7.3 0.8 compare_select_fusion
  8.1 1.7 gather_fusion
  10.1 3.4 fusion.14
  13.6 0.9 scatter_fusion
  14.5 1.3 collective-permute-start.2
  15.9 1.3 collective-permute-start.3
  17.2 5.3 %collective-permute-start = (bf16[128,1664]{1,0:T(8,128)(2,1)S(1)}, bf16[128,1664]{1,0:T(8,128)(2,1)S(1)}, u32[]{:S(2)}, u32[]{:S(2)}) collective-permute-start(bf16[128,1664]{1,0:T(8,128)(2,1)S(1)} %copy-done.6), channel_id=1, source_target_pairs={{0,4},{4,8},{8,12},{12,16},{16,20},{20,24},{24,28},{28,32},{32,36}... | collective-permute-start | bytes 1277960 | tf_op jit(solution)/shard_map/ppermute | solution.py:18
  22.4 1.3 collective-permute-start.1
  23.8 1.0 copy.32
  25.1 0.7 copy-done.7
  25.8 1.2 pad_maximum_fusion.1
  27.0 1.5 copy.31
  28.6 1.1 pad_maximum_fusion
  29.7 1.6 copy.30
  31.3 4.4 %fusion.118 = (f32[16,128]{1,0:T(8,128)S(1)}, f32[16,128,384]{1,2,0:T(8,128)}) fusion(pred[128,384]{0,1:T(8,128)(4,1)S(1)} %broadcast_compare_fusion, bf16[384,16,104]{0,2,1:T(8,128)(2,1)} %bitcast.35, bf16[128,16,104]{0,2,1:T(8,128)(2,1)} %bitcast.38), kind=kOutput, calls=%fused_computation.159 | convolution fusion | flops 166723968 | bytes 4907008 | tf_op jit(solution)/shard_map/sub | solution.py:76
  35.7 2.5 fusion.52
  39.2 6.6 %tile.2 = bf16[32,128,1664]{2,1,0:T(8,128)(2,1)} broadcast(bf16[128,1664]{1,0:T(8,128)(2,1)S(1)} %multiply_convert_fusion), dimensions={1,2} | broadcast | bytes 14057472 | tf_op jit(solution)/shard_map/tile | solution.py:12
  45.8 166.9 %all_to_all.14 = bf16[32,128,1664]{2,1,0:T(8,128)(2,1)} all-to-all(bf16[32,128,1664]{2,1,0:T(8,128)(2,1)} %tile.2), channel_id=1, replica_groups=mesh['blk'=32,'tok'=4] {'blk'}, dimensions={0} | all-to-all | bytes 27262976 | tf_op jit(solution)/shard_map/all_to_all | solution.py:12
  212.7 27.8 %convolution_convert_fusion = bf16[4096,1664]{1,0:T(8,128)(2,1)} fusion(bf16[256,1664]{1,0:T(8,128)(2,1)S(1)} %copy-done, bf16[4096,1664]{1,0:T(8,128)(2,1)} %bitcast.33, bf16[1664,256]{1,0:T(8,128)(2,1)S(1)} %copy-done.15, f32[256]{0:T(256)S(1)} %copy-done.16), kind=kOutput, calls=%fused_computation.3 | convolution fusion | flops 7055343616 | bytes 28967936 | tf_op jit(solution)/shard_map/dot_general | solution.py:87
  241.5 104.7 %reduce-scatter.2.cloned.1.call-done = bf16[128,1664]{1,0:T(8,128)(2,1)} async-done(((bf16[4096,1664]{1,0:T(8,128)(2,1)}), bf16[128,1664]{1,0:T(8,128)(2,1)}) %reduce-scatter.2.cloned.1.call-update) | async-done | bytes 426000 | tf_op jit(solution)/shard_map/reduce_scatter | solution.py:86
  346.2 1.1 convert_add_fusion
  348.5 3.8 %convolution_convert_fusion.1 = bf16[4,32,1664]{2,1,0:T(8,128)(2,1)S(1)} fusion(bf16[1664,1664]{1,0:T(8,128)(2,1)} %param.34, f32[32,1664]{1,0:T(8,128)S(1)} %reduce_sum.87, f32[1664]{0:T(1024)S(1)} %copy-done.12, f32[1664]{0:T(1024)S(1)} %copy-done.13, f32[32]{0:T(128)S(1)} %add_rsqrt_fusion, f32[32]{0:T(128)S(1)} %broadcast_multiply_fusion, ...), kind=kOutput, calls=%fused_computation.27 | convolution fusion | flops 191483904 | bytes 6198144 | tf_op jit(solution)/shard_map/osm,md->osd/dot_general | solution.py:106
  352.3 11.6 %all_to_all.15 = bf16[4,32,1664]{2,1,0:T(8,128)(2,1)S(1)} all-to-all(bf16[4,32,1664]{2,1,0:T(8,128)(2,1)S(1)} %convolution_convert_fusion.1), channel_id=1, replica_groups=mesh['blk'=32,'tok'=4] {'tok'}, dimensions={0} | all-to-all | bytes 851968 | tf_op jit(solution)/shard_map/all_to_all | solution.py:109
  363.9 0.8 copy.40
  (66 shorter events, 3.8 us)
Async XLA Ops:
  7.2 205.5 %copy-start = (bf16[256,1664]{1,0:T(8,128)(2,1)S(1)}, bf16[256,1664]{1,0:T(8,128)(2,1)}, u32[]{:S(2)}) copy-start(bf16[256,1664]{1,0:T(8,128)(2,1)} %param.31) | copy-start | bytes 2555908
  7.2 16.6 %copy-start.8 = (bf16[128,1664]{1,0:T(8,128)(2,1)S(1)}, bf16[128,1664]{1,0:T(8,128)(2,1)}, u32[]{:S(2)}) copy-start(bf16[128,1664]{1,0:T(8,128)(2,1)} %param.19) | copy-start | bytes 1277956
  7.2 6.4 %copy-start.4 = (bf16[128,1664]{1,0:T(8,128)(2,1)S(1)}, bf16[128,1664]{1,0:T(8,128)(2,1)}, u32[]{:S(2)}) copy-start(bf16[128,1664]{1,0:T(8,128)(2,1)} %param.20) | copy-start | bytes 1277956
  7.2 10.0 %copy-start.6 = (bf16[128,1664]{1,0:T(8,128)(2,1)S(1)}, bf16[128,1664]{1,0:T(8,128)(2,1)}, u32[]{:S(2)}) copy-start(bf16[128,1664]{1,0:T(8,128)(2,1)} %param.21) | copy-start | bytes 1277956
  7.2 339.0 %reduce-scatter.2.cloned.1.call-start = ((), (), s32[]{:S(2)}) async-start(), calls=%async_computation.3 | async-start | bytes 14057472 | tf_op jit(solution)/shard_map/reduce_scatter | solution.py:86
  7.3 17.5 %copy-start.10 = (s32[4096]{0:T(1024)S(1)}, s32[4096]{0:T(1024)}, u32[]{:S(2)}) copy-start(s32[4096]{0:T(1024)} %param.22) | copy-start | bytes 49156
  14.5 15.2 %copy-start.3 = (bf16[128,1664]{1,0:T(8,128)(2,1)}, bf16[128,1664]{1,0:T(8,128)(2,1)S(1)}, u32[]{:S(2)}) copy-start(bf16[128,1664]{1,0:T(8,128)(2,1)S(1)} %scatter_fusion) | copy-start | bytes 1277956
  14.5 10.5 %collective-permute-start.2 = (bf16[128,1664]{1,0:T(8,128)(2,1)S(1)}, bf16[128,1664]{1,0:T(8,128)(2,1)S(1)}, u32[]{:S(2)}, u32[]{:S(2)}) collective-permute-start(bf16[128,1664]{1,0:T(8,128)(2,1)S(1)} %scatter_fusion), channel_id=1, source_target_pairs={{0,4},{4,8},{8,12},{12,16},{16,20},{20,24},{24,28},{28,32},{32,36}... | collective-permute-start | bytes 1277960 | tf_op jit(solution)/shard_map/ppermute | solution.py:18
  15.9 9.9 %collective-permute-start.3 = (bf16[128,1664]{1,0:T(8,128)(2,1)S(1)}, bf16[128,1664]{1,0:T(8,128)(2,1)}, u32[]{:S(2)}, u32[]{:S(2)}) collective-permute-start(bf16[128,1664]{1,0:T(8,128)(2,1)S(1)} %scatter_fusion), channel_id=1, source_target_pairs={{4,0},{8,4},{12,8},{16,12},{20,16},{24,20},{28,24},{32,28},{36,32}... | collective-permute-start | bytes 1277960 | tf_op jit(solution)/shard_map/ppermute | solution.py:18
  17.2 11.4 %collective-permute-start = (bf16[128,1664]{1,0:T(8,128)(2,1)S(1)}, bf16[128,1664]{1,0:T(8,128)(2,1)S(1)}, u32[]{:S(2)}, u32[]{:S(2)}) collective-permute-start(bf16[128,1664]{1,0:T(8,128)(2,1)S(1)} %copy-done.6), channel_id=1, source_target_pairs={{0,4},{4,8},{8,12},{12,16},{16,20},{20,24},{24,28},{28,32},{32,36}... | collective-permute-start | bytes 1277960 | tf_op jit(solution)/shard_map/ppermute | solution.py:18
  22.4 6.1 %collective-permute-start.1 = (bf16[128,1664]{1,0:T(8,128)(2,1)S(1)}, bf16[128,1664]{1,0:T(8,128)(2,1)}, u32[]{:S(2)}, u32[]{:S(2)}) collective-permute-start(bf16[128,1664]{1,0:T(8,128)(2,1)S(1)} %copy-done.6), channel_id=1, source_target_pairs={{4,0},{8,4},{12,8},{16,12},{20,16},{24,20},{28,24},{32,28},{36,32}... | collective-permute-start | bytes 1277960 | tf_op jit(solution)/shard_map/ppermute | solution.py:18
  25.0 0.8 copy-start.7
  31.3 4.4 %copy-start.5 = (bf16[384,1664]{0,1:T(8,128)(2,1)S(1)}, bf16[384,1664]{0,1:T(8,128)(2,1)}, u32[]{:S(2)}) copy-start(bf16[384,1664]{0,1:T(8,128)(2,1)} %copy.30) | copy-start | bytes 3833860
  35.7 2.9 copy-start.2
  38.2 0.8 copy-start.11
  45.8 166.9 %copy-start.15 = (bf16[1664,256]{1,0:T(8,128)(2,1)S(1)}, bf16[1664,256]{1,0:T(8,128)(2,1)}, u32[]{:S(2)}) copy-start(bf16[1664,256]{1,0:T(8,128)(2,1)} %param.29) | copy-start | bytes 2555908
  45.8 166.9 %copy-start.16 = (f32[256]{0:T(256)S(1)}, f32[256]{0:T(256)}, u32[]{:S(2)}) copy-start(f32[256]{0:T(256)} %param.30) | copy-start | bytes 3076
  240.5 0.7 copy-start.14
  241.1 106.9 %copy-start.9 = (f32[1664]{0:T(1024)S(1)}, f32[1664]{0:T(1024)}, u32[]{:S(2)}) copy-start(f32[1664]{0:T(1024)} %param.32) | copy-start | bytes 19972
  241.1 107.3 %copy-start.12 = (f32[1664]{0:T(1024)S(1)}, f32[1664]{0:T(1024)}, u32[]{:S(2)}) copy-start(f32[1664]{0:T(1024)} %param.35) | copy-start | bytes 19972
  241.1 107.3 %copy-start.13 = (f32[1664]{0:T(1024)S(1)}, f32[1664]{0:T(1024)}, u32[]{:S(2)}) copy-start(f32[1664]{0:T(1024)} %param.33) | copy-start | bytes 19972
  347.6 17.1 %copy-start.1 = (bf16[256,1664]{1,0:T(8,128)(2,1)S(1)}, bf16[256,1664]{1,0:T(8,128)(2,1)}, u32[]{:S(2)}) copy-start(bf16[256,1664]{1,0:T(8,128)(2,1)} %param.31) | copy-start | bytes 2555908
Sparse Core Ops, SparseCore 0:
  240.6 105.4 reduce-scatter.1
